TPU v7x, 512 devices: a whole 4x8x8 slice. The times are simulated.
512 devices in a mesh: node: 64 (over y_lo, z, core), win: 8 (over y_hi, x).
Axes of the slice: x: 4, y: 8 (y_hi: 2, y_lo: 4; y = y_hi * 4 + y_lo), z: 8, core: 2. Of those that a mesh axis runs over, the one named last changes fastest.
Arguments:
- features: bfloat16 [32768, 8, 2, 128], P('node', 'win'), may hold values from -6 to 6
- node_vectors: float32 [32768, 128], P('node'), may hold values from -0.3 to 0.3
- projections: float32 [2, 64, 64], replicated, may hold values from -0.75 to 0.75
- mix_weight: bfloat16 [3, 128, 128], replicated, may hold values from -0.3125 to 0.3125
- region_sizes: int32 [128], replicated, may hold values from 1 to 4, 256 in all
- cotangent: bfloat16 [32768, 8, 2, 128], P('node', 'win'), may hold values from -6 to 6
Outputs:
- layer_output: bfloat16 [32768, 8, 2, 128], P('node', 'win')
- vector_grad: float32 [32768, 128], P('node')
- weight_grad: float32 [3, 128, 128], replicated
Inputs may be any that keep to these rules, and one draw needn't show every extreme that they name: `region_sizes`: each entry is a region size in units of 128 nodes; the entries sum to 256, and the largest region has 512 nodes.
All inputs are finite; a program needn't handle non-finite values.
Results may differ from a plain program's by a relative error of at most 0.015.
Values may be sent and summed in bfloat16 or wider, within the bound.
No kernel may reach another device: no remote copies, remote signals or barrier semaphores. Data moves between devices by JAX's collectives and lax.ppermute only.
A program may use at most 64 MiB of HBM per device.

v0:
```python
from functools import partial
import math

import jax
import jax.numpy as jnp
from jax import lax
from jax.experimental import pallas as pl
from jax.experimental.pallas import tpu as pltpu
from jax.sharding import PartitionSpec as P


BLOCK = 128
HALO = 3
KEEP_INPUT = 0.05
F32 = jnp.float32
BF16 = jnp.bfloat16
NT = (((1,), (1,)), ((), ()))
TN = (((0,), (0,)), ((), ()))


def block_diagonal(projections):
    zero = jnp.zeros_like(projections[0])
    return jnp.concatenate(
        [
            jnp.concatenate([projections[0], zero], axis=1),
            jnp.concatenate([zero, projections[1]], axis=1),
        ],
        axis=0,
    )


def split_product(left, right, dims):
    (left_axis,), (right_axis,) = dims[0]
    high, other = left.astype(BF16), right.astype(BF16)
    low = (left - high.astype(F32)).astype(BF16)
    rest = (right - other.astype(F32)).astype(BF16)
    return lax.dot_general(
        jnp.concatenate([high, high, low], axis=left_axis),
        jnp.concatenate([other, rest, other], axis=right_axis),
        dims,
        preferred_element_type=F32,
    )


def pack_kernel(
    x_hbm, g_hbm, nv_hbm, proj_hbm, mix_hbm, own_ref, far_ref, near_ref, m_ref, proj_ref, mix_ref,
    x_in, g_in, nv_in, flat_ref, sems,
):
    copies = [
        pltpu.make_async_copy(source, target, sems.at[i])
        for i, (source, target) in enumerate(
            (
                (x_hbm, x_in),
                (g_hbm, g_in),
                (nv_hbm, nv_in),
                (proj_hbm, proj_ref),
                (mix_hbm, mix_ref),
            )
        )
    ]
    for copy in copies:
        copy.start()
    nodes, width = m_ref.shape
    rim = far_ref.shape[0]
    for part, source in enumerate((x_in, g_in)):
        copies[part].wait()
        flat_ref[...] = source[...].astype(F32)
        for step in range(2):
            rows = flat_ref[pl.ds(step, nodes, stride=2), :].astype(BF16)
            first = (1 + 2 * part + step) * width
            own_ref[:, first : first + width] = rows
    copies[2].wait()
    copies[3].wait()
    learned = jnp.tanh(
        3.0 * split_product(nv_in[...], block_diagonal(proj_ref[...]), (((1,), (0,)), ((), ())))
    )
    m_ref[...] = learned
    own_ref[:, :width] = learned.astype(BF16)
    odd = lax.rem(lax.axis_index("node"), 2)
    gap = nodes - rim
    far_ref[...] = own_ref[pl.ds(pl.multiple_of(odd * gap, BLOCK), rim), :]
    near_ref[...] = own_ref[pl.ds(pl.multiple_of((1 - odd) * gap, BLOCK), rim), :]
    copies[4].wait()


def unit_rows(first, count=1):
    return slice(first * BLOCK, (first + count) * BLOCK)


def rim_places(rim, nodes):
    odd = lax.rem(lax.axis_index("node"), 2)
    span = rim + nodes
    return (
        pl.ds(pl.multiple_of(odd * span, BLOCK), rim),
        pl.ds(pl.multiple_of((1 - odd) * span, BLOCK), rim),
    )


def beside(left, right):
    return jnp.concatenate([left, right], axis=1)


def twice(values):
    return beside(values, values)


def turned(learned):
    width = learned.shape[1]
    half = width // 2
    i = lax.broadcasted_iota(jnp.int32, (width, width), 0)
    j = lax.broadcasted_iota(jnp.int32, (width, width), 1)
    turn = jnp.where(i == j + half, 1.0, 0.0) - jnp.where(j == i + half, 1.0, 0.0)
    return jnp.dot(learned, turn.astype(BF16), preferred_element_type=F32).astype(BF16)


def layer_kernel(
    norm_scale,
    region_ref,
    first_ref,
    far_ref,
    near_ref,
    own_ref,
    m_ref,
    proj_ref,
    mix_ref,
    out_hbm,
    sums_ref,
    x_ref,
    g_ref,
    learned_ref,
    swapped_ref,
    adj_ref,
    adjt_ref,
    score_ref,
    rdeg_ref,
    one_ref,
    two_ref,
    q_one_ref,
    q_two_ref,
    back_ref,
    off_ref,
    offrow_ref,
    dm_ref,
    flat_ref,
    out_ref,
    sem,
):
    b = BLOCK
    nodes = own_ref.shape[0]
    rim, width = far_ref.shape[0], m_ref.shape[1]
    own_units = nodes // b
    units = own_units + 2 * HALO
    reach = HALO + 1
    row = 2 * width
    keep = 1.0 - KEEP_INPUT
    far_place, near_place = rim_places(rim, nodes)
    own_place = pl.ds(rim, nodes)
    for place, source in ((far_place, far_ref), (own_place, own_ref), (near_place, near_ref)):
        learned = source[:, :width]
        learned_ref[place, :] = learned
        swapped_ref[place, :] = turned(learned)
        x_ref[place, :] = source[:, width : width + row]
        g_ref[place, :] = source[:, width + row :]

    firsts = [first_ref[u] for u in range(units)]
    windows = [pl.ds(pl.multiple_of(firsts[u] * b, b), reach * b) for u in range(units)]
    own_first = HALO
    own_last = own_first + own_units
    mixed = jnp.concatenate([mix_ref[2], mix_ref[1]], axis=0)
    for u in range(units):
        rows = unit_rows(u)
        mine = region_ref[u]
        total = jnp.zeros((b, b), F32)
        for k in range(0, reach, 2):
            other = firsts[u] + k
            pair_scores = lax.dot_general(
                learned_ref[rows, :],
                swapped_ref[pl.ds(pl.multiple_of(other * b, b), 2 * b), :],
                NT,
                preferred_element_type=F32,
            )
            for i in range(2):
                same = jnp.where((region_ref[other + i] == mine) & (mine >= 0), 3.0, 0.0)
                squashed = jnp.tanh(pair_scores[:, i * b : (i + 1) * b] * same)
                positive = jnp.maximum(squashed, 0.0)
                negative = jnp.minimum(squashed, 0.0)
                forward = positive * positive
                columns = unit_rows(k + i)
                if own_first <= u < own_last:
                    score_ref[unit_rows(u - own_first), columns] = squashed
                adj_ref[rows, columns] = forward.astype(BF16)
                adjt_ref[rows, columns] = (negative * negative).astype(BF16)
                total = total + forward
        degree = 1.0 + jnp.sum(total, axis=1, keepdims=True)
        rdeg = jnp.broadcast_to(1.0 / degree, (b, width))
        rdeg_ref[rows, :] = rdeg
        for s in range(2):
            cut = slice(s * width, (s + 1) * width)
            back = lax.dot_general(g_ref[rows, cut], mixed, NT, preferred_element_type=F32)
            q_two_ref[rows, cut] = (keep * back[:, :width] * rdeg).astype(BF16)
            back_ref[rows, cut] = back[:, width:]
    order = list(range(own_first, own_last))
    order += [u for u in range(units) if u not in order]
    for u in order:
        rows = unit_rows(u)
        rdeg = twice(rdeg_ref[rows, :])
        carried = jnp.dot(
            adjt_ref[rows, :], q_two_ref[windows[u], :], preferred_element_type=F32
        )
        mine = x_ref[rows, :].astype(F32)
        prop = jnp.dot(adj_ref[rows, :], x_ref[windows[u], :], preferred_element_type=F32)
        prop = (prop + mine) * rdeg
        one_ref[rows, :] = (KEEP_INPUT * mine + keep * prop).astype(BF16)
        carried = carried + q_two_ref[rows, :].astype(F32)
        grad_one = (keep * (back_ref[rows, :] + carried) * rdeg).astype(BF16)
        q_one_ref[rows, :] = grad_one
        inner = grad_one.astype(F32) * prop
        off_ref[rows, :] = inner[:, :width] + inner[:, width:]

    def second_hop(u):
        rows = unit_rows(u)
        prop = jnp.dot(adj_ref[rows, :], one_ref[windows[u], :], preferred_element_type=F32)
        prop = (prop + one_ref[rows, :].astype(F32)) * twice(rdeg_ref[rows, :])
        inner = q_two_ref[rows, :].astype(F32) * prop
        inner = off_ref[rows, :] + inner[:, :width] + inner[:, width:]
        offset = jnp.broadcast_to(jnp.sum(inner, axis=1, keepdims=True), (b, width))
        off_ref[rows, :] = offset
        offrow_ref[u] = jnp.transpose(offset)[:8]
        if own_first <= u < own_last:
            two_ref[unit_rows(u - own_first), :] = (
                KEEP_INPUT * x_ref[rows, :].astype(F32) + keep * prop
            ).astype(BF16)

    for u in range(own_first, own_last):
        second_hop(u)
    weights = jnp.concatenate([mix_ref[0], mix_ref[1], mix_ref[2]], axis=0)
    all_hops, all_up = [], []
    for s in range(2):
        cut = slice(s * width, (s + 1) * width)
        all_hops.append(
            jnp.concatenate(
                [x_ref[own_place, cut], one_ref[own_place, cut], two_ref[:, cut]], axis=1
            )
        )
        all_up.append(g_ref[own_place, cut])
        flat_ref[pl.ds(s, nodes, stride=2), :] = jnp.dot(
            all_hops[s], weights, preferred_element_type=F32
        )
    out_ref[...] = flat_ref[...].astype(BF16)
    out_copy = pltpu.make_async_copy(out_ref, out_hbm, sem)
    out_copy.start()
    for u in range(units):
        if not own_first <= u < own_last:
            second_hop(u)
    groups = sums_ref.shape[0]
    rows_v = nodes // groups
    rows_w = 3 * width // groups
    weight = norm_scale * lax.dot_general(
        jnp.concatenate(all_hops, axis=0),
        jnp.concatenate(all_up, axis=0),
        TN,
        preferred_element_type=F32,
    )
    for k in range(groups):
        sums_ref[k, rows_v:, :] = weight[k * rows_w : (k + 1) * rows_w].astype(BF16)

    for u in range(own_first, own_last):
        rows = unit_rows(u)
        local = unit_rows(u - own_first)
        grad_m = jnp.zeros((b, width), F32)
        for k in range(0, reach, 2):
            columns = pl.ds(pl.multiple_of((firsts[u] + k) * b, b), 2 * b)
            inner = lax.dot_general(
                beside(q_one_ref[rows, :], q_two_ref[rows, :]),
                beside(x_ref[columns, :], one_ref[columns, :]),
                NT,
                preferred_element_type=F32,
            )
            inner_t = lax.dot_general(
                beside(x_ref[rows, :], one_ref[rows, :]),
                beside(q_one_ref[columns, :], q_two_ref[columns, :]),
                NT,
                preferred_element_type=F32,
            )
            squashed = score_ref[local, unit_rows(k, 2)]
            offset_t = jnp.concatenate(
                [offrow_ref[firsts[u] + k + i, 0:1, :] for i in range(2)], axis=1
            )
            chosen = jnp.where(
                squashed > 0.0, inner - twice(off_ref[rows, :]), inner_t - offset_t
            )
            pair = (6.0 * squashed * (1.0 - squashed * squashed) * chosen).astype(BF16)
            grad_m = grad_m + jnp.dot(
                pair, swapped_ref[columns, :], preferred_element_type=F32
            )
        mine = m_ref[local, :]
        dm_ref[local, :] = 3.0 * (1.0 - mine * mine) * grad_m
    grad = split_product(dm_ref[...], block_diagonal(proj_ref[...]), NT).astype(BF16)
    for k in range(groups):
        sums_ref[k, :rows_v, :] = grad[k * rows_v : (k + 1) * rows_v]
    out_copy.wait()


def finish_kernel(got_ref, vector_ref, weight_ref):
    groups = got_ref.shape[0]
    rows_v = vector_ref.shape[0] // groups
    rows_w = weight_ref.shape[0] // groups
    for k in range(groups):
        got = got_ref[k].astype(F32)
        vector_ref[k * rows_v : (k + 1) * rows_v, :] = got[:rows_v]
        weight_ref[k * rows_w : (k + 1) * rows_w, :] = got[rows_v:]


def device_groups(counts, kept):
    strides = [math.prod(counts[i + 1 :]) for i in range(len(counts))]

    def spread(axes):
        numbers = [0]
        for i in axes:
            numbers = [n + k * strides[i] for n in numbers for k in range(counts[i])]
        return numbers

    others = [i for i in range(len(counts)) if i not in kept]
    return [[base + k for k in spread(kept)] for base in spread(others)]


def body(features, node_vectors, projections, mix_weight, region_sizes, cotangent):
    nodes, _, steps, width = features.shape
    axes = ("node", "win")
    node_count, win_count = lax.axis_size("node"), lax.axis_size("win")
    own_units = nodes // BLOCK
    units = own_units + 2 * HALO
    rim = HALO * BLOCK
    flat = nodes * steps
    row = steps * width
    in_vmem = pl.BlockSpec(memory_space=pltpu.VMEM)
    in_hbm = pl.BlockSpec(memory_space=pltpu.HBM)
    features, cotangent = features.reshape(flat, width), cotangent.reshape(flat, width)
    features, cotangent, node_vectors, projections, mix_weight = (
        pltpu.with_memory_space_constraint(array, pltpu.HBM)
        for array in (features, cotangent, node_vectors, projections, mix_weight)
    )
    own, far, near, learned, projections, mix_weight = pl.pallas_call(
        pack_kernel,
        name="pack",
        in_specs=[in_hbm] * 5,
        out_shape=(
            jax.ShapeDtypeStruct((nodes, 5 * width), BF16),
            jax.ShapeDtypeStruct((rim, 5 * width), BF16),
            jax.ShapeDtypeStruct((rim, 5 * width), BF16),
            jax.ShapeDtypeStruct((nodes, width), F32),
            jax.ShapeDtypeStruct(projections.shape, F32),
            jax.ShapeDtypeStruct(mix_weight.shape, BF16),
        ),
        scratch_shapes=[
            pltpu.VMEM((flat, width), BF16),
            pltpu.VMEM((flat, width), BF16),
            pltpu.VMEM((nodes, width), F32),
            pltpu.VMEM((flat, width), F32),
            pltpu.SemaphoreType.DMA((5,)),
        ],
        compiler_params=pltpu.CompilerParams(vmem_limit_bytes=16 << 20),
    )(features, cotangent, node_vectors, projections, mix_weight)
    border = [(i, i + 1) for i in range(1, node_count - 1, 2)]
    inside = [(i, i + 1) for i in range(0, node_count, 2)]
    far = lax.ppermute(far, "node", border + [(j, i) for i, j in border])
    near = lax.ppermute(near, "node", inside + [(j, i) for i, j in inside])
    lead = lax.axis_index("node") * own_units - HALO
    place = jnp.arange(units, dtype=jnp.int32)
    unit = lead + place
    ends = jnp.cumsum(region_sizes)
    passed = (ends[None, :] <= unit[:, None]).astype(jnp.int32)
    in_range = (unit >= 0) & (unit < node_count * own_units)
    region = jnp.where(in_range, jnp.sum(passed, axis=1), -1)
    first = jnp.sum(passed * region_sizes[None, :], axis=1) - lead
    first = jnp.clip(first, jnp.maximum(place - HALO, 0), jnp.minimum(place, units - HALO - 1))

    span = units * BLOCK
    y_far, y_near = 4, 1
    inner_count = node_count // (y_far * y_near)
    groups = y_far * win_count
    rows_v = nodes // groups
    rows_w = 3 * width // groups
    reach = (HALO + 1) * BLOCK
    in_smem = pl.BlockSpec(memory_space=pltpu.SMEM)
    out, sums = pl.pallas_call(
        partial(layer_kernel, 1.0 / math.sqrt(flat * node_count * win_count)),
        name="layer",
        in_specs=[in_smem] * 2 + [in_vmem] * 6,
        out_specs=(in_hbm, in_vmem),
        out_shape=(
            jax.ShapeDtypeStruct((flat, width), BF16),
            jax.ShapeDtypeStruct((groups, rows_v + rows_w, width), BF16),
        ),
        scratch_shapes=[
            pltpu.VMEM((span, row), BF16),
            pltpu.VMEM((span, row), BF16),
            pltpu.VMEM((span, width), BF16),
            pltpu.VMEM((span, width), BF16),
            pltpu.VMEM((span, reach), BF16),
            pltpu.VMEM((span, reach), BF16),
            pltpu.VMEM((nodes, reach), F32),
            pltpu.VMEM((span, width), F32),
            pltpu.VMEM((span, row), BF16),
            pltpu.VMEM((nodes, row), BF16),
            pltpu.VMEM((span, row), BF16),
            pltpu.VMEM((span, row), BF16),
            pltpu.VMEM((span, row), F32),
            pltpu.VMEM((span, width), F32),
            pltpu.VMEM((units, 8, width), F32),
            pltpu.VMEM((nodes, width), F32),
            pltpu.VMEM((flat, width), F32),
            pltpu.VMEM((flat, width), BF16),
            pltpu.SemaphoreType.DMA,
        ],
        compiler_params=pltpu.CompilerParams(vmem_limit_bytes=32 << 20),
        cost_estimate=pl.CostEstimate(
            flops=12 * span * reach * row, bytes_accessed=8 << 20, transcendentals=span * reach
        ),
    )(region, first, far, near, own, learned, projections, mix_weight)

    counts = (y_far, y_near, inner_count, win_count)
    outer_groups = device_groups(counts, (0, 3))
    inner_groups = device_groups(counts, (1, 2))
    exchange = partial(
        lax.all_to_all, axis_name=axes, split_axis=0, concat_axis=0, tiled=True
    )
    got = exchange(sums, axis_index_groups=outer_groups).astype(F32)
    vector_sum = jnp.sum(
        got[:, :rows_v].reshape(y_far, win_count, rows_v, width), axis=1
    ).astype(BF16)
    weight_sum = jnp.sum(got[:, rows_v:], axis=0).astype(BF16)
    shares = jnp.broadcast_to(weight_sum[None], (y_near * inner_count, rows_w, width))
    vector_sum, shares = lax.optimization_barrier((vector_sum, shares))
    got = exchange(shares, axis_index_groups=inner_groups).astype(F32)
    weight_sum = jnp.sum(got, axis=0).astype(BF16)
    back = jnp.concatenate(
        [
            jnp.broadcast_to(
                vector_sum[:, None], (y_far, win_count, rows_v, width)
            ).reshape(groups, rows_v, width),
            jnp.broadcast_to(weight_sum[None], (groups, rows_w, width)),
        ],
        axis=1,
    )
    got = exchange(back, axis_index_groups=outer_groups)
    vector_grad, weight_grad = pl.pallas_call(
        finish_kernel,
        name="finish",
        in_specs=[in_vmem],
        out_shape=(
            jax.ShapeDtypeStruct((nodes, width), F32),
            jax.ShapeDtypeStruct((3 * width, width), F32),
        ),
        compiler_params=pltpu.CompilerParams(vmem_limit_bytes=8 << 20),
    )(got)
    weight_grad = weight_grad.reshape(3, width, width)
    return (out.reshape(nodes, 1, steps, width), vector_grad, weight_grad)


def solution(mesh):
    placed = (
        P("node", "win", None, None),
        P("node", None),
        P(),
        P(),
        P(),
        P("node", "win", None, None),
    )
    return jax.shard_map(
        body,
        mesh=mesh,
        in_specs=placed,
        out_specs=(P("node", "win", None, None), P("node", None), P()),
        check_vma=False,
    )
```

profile of v0, /device:TPU:1, one launch (start us, length us, event | category | flops | bytes accessed | tf_op | source)
XLA Modules:
  0.0 78.3 jit_solution(14959020679009501564)
XLA Ops:
  0.6 1.6 %pack.1 = (bf16[512,640]{1,0:T(8,128)(2,1)S(1)}, bf16[384,640]{1,0:T(8,128)(2,1)S(1)}, bf16[384,640]{1,0:T(8,128)(2,1)S(1)}, f32[512,128]{1,0:T(8,128)S(1)}, f32...) custom-call(bf16[1024,128]{1,0:T(8,128)(2,1)} %bitcast.11, bf16[1024,128]{1,0:T(8,128)(2,1)} %bitcast.12, ...), custom_call_target="tpu_custom_call" | custom-call | tf_op jit(solution)/shard_map/pack/pallas_call | solution.py:343
  2.2 5.4 %collective-permute-start = (bf16[384,640]{1,0:T(8,128)(2,1)S(1)}, bf16[384,640]{1,0:T(8,128)(2,1)S(1)}, u32[]{:S(2)}, u32[]{:S(2)}) collective-permute-start(bf16[384,640]{1,0:T(8,128)(2,1)S(1)} %get-tuple-element.15), channel_id=1, source_target_pairs={{8,16},{24,32},{40,48},{56,64},{72,80},{88,96},{104,112},{120,128}... | collective-permute-start | bytes 1474568 | tf_op jit(solution)/shard_map/ppermute | solution.py:366
  7.6 4.1 %collective-permute-start.1 = (bf16[384,640]{1,0:T(8,128)(2,1)S(1)}, bf16[384,640]{1,0:T(8,128)(2,1)S(1)}, u32[]{:S(2)}, u32[]{:S(2)}) collective-permute-start(bf16[384,640]{1,0:T(8,128)(2,1)S(1)} %get-tuple-element.16), channel_id=1, source_target_pairs={{0,8},{16,24},{32,40},{48,56},{64,72},{80,88},{96,104},{112,120},{... | collective-permute-start | bytes 1474568 | tf_op jit(solution)/shard_map/ppermute | solution.py:367
  11.7 0.0 copy-start
  11.7 0.6 copy-done
  12.3 0.1 copy.15
  12.4 0.2 reduce-window.8
  12.6 0.1 reduce.1
  12.7 0.2 fusion.1
  12.9 1.2 %collective-permute-done.far_ref = bf16[384,640]{1,0:T(8,128)(2,1)S(1)} collective-permute-done((bf16[384,640]{1,0:T(8,128)(2,1)S(1)}, bf16[384,640]{1,0:T(8,128)(2,1)S(1)}, u32[]{:S(2)}, u32[]{:S(2)}) %collective-permute-start) | collective-permute-done | bytes 491552 | tf_op jit(solution)/shard_map/ppermute | solution.py:366
  14.1 0.0 collective-permute-done.1.near_ref
  14.1 5.9 %layer.1 = (bf16[1024,128]{1,0:T(8,128)(2,1)}, bf16[32,28,128]{2,1,0:T(8,128)(2,1)S(1)}) custom-call(s32[10]{0:T(128)S(1)} %get-tuple-element.41.region_ref, s32[10]{0:T(128)S(1)} %get-tuple-element.42.first_ref, bf16[384,640]{1,0:T(8,128)(2,1)S(1)} %collective-permute-done.far_ref, bf16[384,640]{1,0:T(8,128)(2,1)S(1)} %collective-permute-done.1.near_ref, ...), custom_call_target="tpu_custom_call" | custom-call | flops 2013265920 | bytes 8388608 | tf_op jit(solution)/shard_map/layer/pallas_call | solution.py:386
  20.0 23.5 %all_to_all.15 = bf16[32,28,128]{2,1,0:T(8,128)(2,1)S(1)} all-to-all(bf16[32,28,128]{2,1,0:T(8,128)(2,1)S(1)} %get-tuple-element.22), channel_id=1, replica_groups={{0,1,2,3,4,5,6,7,128,129,130,131,132,133,134,135,256,257,258,259,260,26..., dimensions={0} | all-to-all | bytes 458752 | tf_op jit(solution)/shard_map/all_to_all | solution.py:428
  43.5 0.1 convert_element_type.19
  43.6 18.0 %all_to_all.16 = bf16[16,12,128]{2,1,0:T(8,128)(2,1)S(1)} all-to-all(bf16[16,12,128]{2,1,0:T(8,128)(2,1)S(1)} %broadcast_in_dim.11), channel_id=1, replica_groups={{0,8,16,24,32,40,48,56,64,72,80,88,96,104,112,120},{1,9,17,25,33,41,49,..., dimensions={0} | all-to-all | bytes 98304 | tf_op jit(solution)/shard_map/all_to_all | solution.py:435
  61.8 15.7 %all_to_all.17.got_ref = bf16[32,28,128]{2,1,0:T(8,128)(2,1)S(1)} all-to-all(bf16[32,28,128]{2,1,0:T(8,128)(2,1)S(1)} %pad_maximum_fusion), channel_id=1, replica_groups={{0,1,2,3,4,5,6,7,128,129,130,131,132,133,134,135,256,257,258,259,260,26..., dimensions={0} | all-to-all | bytes 458752 | tf_op jit(solution)/shard_map/all_to_all | solution.py:446
  77.5 0.8 %finish.1 = (f32[512,128]{1,0:T(8,128)}, f32[384,128]{1,0:T(8,128)}) custom-call(bf16[32,28,128]{2,1,0:T(8,128)(2,1)S(1)} %all_to_all.17.got_ref), custom_call_target="tpu_custom_call" | custom-call | tf_op jit(solution)/shard_map/finish/pallas_call | solution.py:447
  (9 shorter events, 0.2 us)
Async XLA Ops:
  2.2 11.9 %collective-permute-start = (bf16[384,640]{1,0:T(8,128)(2,1)S(1)}, bf16[384,640]{1,0:T(8,128)(2,1)S(1)}, u32[]{:S(2)}, u32[]{:S(2)}) collective-permute-start(bf16[384,640]{1,0:T(8,128)(2,1)S(1)} %get-tuple-element.15), channel_id=1, source_target_pairs={{8,16},{24,32},{40,48},{56,64},{72,80},{88,96},{104,112},{120,128}... | collective-permute-start | bytes 1474568 | tf_op jit(solution)/shard_map/ppermute | solution.py:366
  7.6 6.5 %collective-permute-start.1 = (bf16[384,640]{1,0:T(8,128)(2,1)S(1)}, bf16[384,640]{1,0:T(8,128)(2,1)S(1)}, u32[]{:S(2)}, u32[]{:S(2)}) collective-permute-start(bf16[384,640]{1,0:T(8,128)(2,1)S(1)} %get-tuple-element.16), channel_id=1, source_target_pairs={{0,8},{16,24},{32,40},{48,56},{64,72},{80,88},{96,104},{112,120},{... | collective-permute-start | bytes 1474568 | tf_op jit(solution)/shard_map/ppermute | solution.py:367
  11.7 0.7 copy-start
where the time goes:
time: 78.6 us; the launch traced here: 78.3 us
  blocking collectives  57.3 us (73%)
  starting transfers between devices  9.43 us (12%)
  Pallas kernels  8.23 us (10%)
  waiting for transfers between devices  1.17 us (1%)
  local copies, waits for them, and re-layouts  0.81 us (1%)
    all_to_all x1, blocking collectives, body(): got = exchange(sums, axis_index_groups=outer_groups).astype(F32)  23.5 us
    all_to_all x1, blocking collectives, body(): got = exchange(shares, axis_index_groups=inner_groups).astype(F32)  18 us
    all_to_all x1, blocking collectives, body(): got = exchange(back, axis_index_groups=outer_groups)  15.7 us
    pallas_call x1, Pallas kernels, body(): pl.pallas_call(partial(layer_kernel, 1.0 / math.sqrt(flat * node_count *...  5.85 us
    ppermute x1, starting transfers between devices, body(): far = lax.ppermute(far, 'node', border + [(j, i) for i, j in border])  5.37 us
    ppermute x1, starting transfers between devices, body(): near = lax.ppermute(near, 'node', inside + [(j, i) for i, j in inside])  4.06 us
    pallas_call x1, Pallas kernels, body(): pl.pallas_call(pack_kernel, name='pack', in_specs=[in_hbm] * 5, out_shape...  1.58 us
  transfers between devices with their start and end apart: 2, of which 1 were waited for; matrix products, arithmetic and copies ran while one was open for 1% of the time, Pallas kernels for 0%

commit v1 on v0

--- a/solution.py
+++ b/solution.py
@@ -301,7 +301,7 @@
     out_copy.wait()
 
 
-def finish_kernel(got_ref, vector_ref, weight_ref):
+def finish_kernel(got_ref, vector_hbm, weight_hbm, vector_ref, weight_ref, sems):
     groups = got_ref.shape[0]
     rows_v = vector_ref.shape[0] // groups
     rows_w = weight_ref.shape[0] // groups
@@ -309,6 +309,14 @@
         got = got_ref[k].astype(F32)
         vector_ref[k * rows_v : (k + 1) * rows_v, :] = got[:rows_v]
         weight_ref[k * rows_w : (k + 1) * rows_w, :] = got[rows_v:]
+    copies = (
+        pltpu.make_async_copy(vector_ref, vector_hbm, sems.at[0]),
+        pltpu.make_async_copy(weight_ref, weight_hbm, sems.at[1]),
+    )
+    for copy in copies:
+        copy.start()
+    for copy in copies:
+        copy.wait()
 
 
 def device_groups(counts, kept):
@@ -452,6 +460,12 @@
             jax.ShapeDtypeStruct((nodes, width), F32),
             jax.ShapeDtypeStruct((3 * width, width), F32),
         ),
+        out_specs=(in_hbm, in_hbm),
+        scratch_shapes=[
+            pltpu.VMEM((nodes, width), F32),
+            pltpu.VMEM((3 * width, width), F32),
+            pltpu.SemaphoreType.DMA((2,)),
+        ],
         compiler_params=pltpu.CompilerParams(vmem_limit_bytes=8 << 20),
     )(got)
     weight_grad = weight_grad.reshape(3, width, width)

time: 78.6 us -> 78.6 us (level)
  no operation moved by 1% of the time
where the time goes in v1:
time: 78.6 us; the launch traced here: 78.3 us
  blocking collectives  57.3 us (73%)
  starting transfers between devices  9.43 us (12%)
  Pallas kernels  8.23 us (10%)
  waiting for transfers between devices  1.17 us (1%)
  local copies, waits for them, and re-layouts  0.81 us (1%)
    all_to_all x1, blocking collectives, body(): got = exchange(sums, axis_index_groups=outer_groups).astype(F32)  23.5 us
    all_to_all x1, blocking collectives, body(): got = exchange(shares, axis_index_groups=inner_groups).astype(F32)  18 us
    all_to_all x1, blocking collectives, body(): got = exchange(back, axis_index_groups=outer_groups)  15.7 us
    pallas_call x1, Pallas kernels, body(): pl.pallas_call(partial(layer_kernel, 1.0 / math.sqrt(flat * node_count *...  5.85 us
    ppermute x1, starting transfers between devices, body(): far = lax.ppermute(far, 'node', border + [(j, i) for i, j in border])  5.37 us
    ppermute x1, starting transfers between devices, body(): near = lax.ppermute(near, 'node', inside + [(j, i) for i, j in inside])  4.06 us
    pallas_call x1, Pallas kernels, body(): pl.pallas_call(pack_kernel, name='pack', in_specs=[in_hbm] * 5, out_shape...  1.58 us
  transfers between devices with their start and end apart: 2, of which 1 were waited for; matrix products, arithmetic and copies ran while one was open for 1% of the time, Pallas kernels for 0%

profile of v1, /device:TPU:1, one launch (start us, length us, event | category | flops | bytes accessed | tf_op | source)
XLA Modules:
  0.0 78.3 jit_solution(168485107302550975)
XLA Ops:
  0.6 1.6 %pack.1 = (bf16[512,640]{1,0:T(8,128)(2,1)S(1)}, bf16[384,640]{1,0:T(8,128)(2,1)S(1)}, bf16[384,640]{1,0:T(8,128)(2,1)S(1)}, f32[512,128]{1,0:T(8,128)S(1)}, f32...) custom-call(bf16[1024,128]{1,0:T(8,128)(2,1)} %bitcast.11, bf16[1024,128]{1,0:T(8,128)(2,1)} %bitcast.12, ...), custom_call_target="tpu_custom_call" | custom-call | tf_op jit(solution)/shard_map/pack/pallas_call | solution.py:351
  2.2 5.4 %collective-permute-start = (bf16[384,640]{1,0:T(8,128)(2,1)S(1)}, bf16[384,640]{1,0:T(8,128)(2,1)S(1)}, u32[]{:S(2)}, u32[]{:S(2)}) collective-permute-start(bf16[384,640]{1,0:T(8,128)(2,1)S(1)} %get-tuple-element.15), channel_id=1, source_target_pairs={{8,16},{24,32},{40,48},{56,64},{72,80},{88,96},{104,112},{120,128}... | collective-permute-start | bytes 1474568 | tf_op jit(solution)/shard_map/ppermute | solution.py:374
  7.6 4.1 %collective-permute-start.1 = (bf16[384,640]{1,0:T(8,128)(2,1)S(1)}, bf16[384,640]{1,0:T(8,128)(2,1)S(1)}, u32[]{:S(2)}, u32[]{:S(2)}) collective-permute-start(bf16[384,640]{1,0:T(8,128)(2,1)S(1)} %get-tuple-element.16), channel_id=1, source_target_pairs={{0,8},{16,24},{32,40},{48,56},{64,72},{80,88},{96,104},{112,120},{... | collective-permute-start | bytes 1474568 | tf_op jit(solution)/shard_map/ppermute | solution.py:375
  11.7 0.0 copy-start
  11.7 0.6 copy-done
  12.3 0.1 copy.15
  12.4 0.2 reduce-window.8
  12.6 0.1 reduce.1
  12.7 0.2 fusion.1
  12.9 1.2 %collective-permute-done.far_ref = bf16[384,640]{1,0:T(8,128)(2,1)S(1)} collective-permute-done((bf16[384,640]{1,0:T(8,128)(2,1)S(1)}, bf16[384,640]{1,0:T(8,128)(2,1)S(1)}, u32[]{:S(2)}, u32[]{:S(2)}) %collective-permute-start) | collective-permute-done | bytes 491552 | tf_op jit(solution)/shard_map/ppermute | solution.py:374
  14.1 0.0 collective-permute-done.1.near_ref
  14.1 5.9 %layer.1 = (bf16[1024,128]{1,0:T(8,128)(2,1)}, bf16[32,28,128]{2,1,0:T(8,128)(2,1)S(1)}) custom-call(s32[10]{0:T(128)S(1)} %get-tuple-element.41.region_ref, s32[10]{0:T(128)S(1)} %get-tuple-element.42.first_ref, bf16[384,640]{1,0:T(8,128)(2,1)S(1)} %collective-permute-done.far_ref, bf16[384,640]{1,0:T(8,128)(2,1)S(1)} %collective-permute-done.1.near_ref, ...), custom_call_target="tpu_custom_call" | custom-call | flops 2013265920 | bytes 8388608 | tf_op jit(solution)/shard_map/layer/pallas_call | solution.py:394
  20.0 23.5 %all_to_all.15 = bf16[32,28,128]{2,1,0:T(8,128)(2,1)S(1)} all-to-all(bf16[32,28,128]{2,1,0:T(8,128)(2,1)S(1)} %get-tuple-element.22), channel_id=1, replica_groups={{0,1,2,3,4,5,6,7,128,129,130,131,132,133,134,135,256,257,258,259,260,26..., dimensions={0} | all-to-all | bytes 458752 | tf_op jit(solution)/shard_map/all_to_all | solution.py:436
  43.5 0.1 convert_element_type.19
  43.6 18.0 %all_to_all.16 = bf16[16,12,128]{2,1,0:T(8,128)(2,1)S(1)} all-to-all(bf16[16,12,128]{2,1,0:T(8,128)(2,1)S(1)} %broadcast_in_dim.11), channel_id=1, replica_groups={{0,8,16,24,32,40,48,56,64,72,80,88,96,104,112,120},{1,9,17,25,33,41,49,..., dimensions={0} | all-to-all | bytes 98304 | tf_op jit(solution)/shard_map/all_to_all | solution.py:443
  61.8 15.7 %all_to_all.17.got_ref = bf16[32,28,128]{2,1,0:T(8,128)(2,1)S(1)} all-to-all(bf16[32,28,128]{2,1,0:T(8,128)(2,1)S(1)} %pad_maximum_fusion), channel_id=1, replica_groups={{0,1,2,3,4,5,6,7,128,129,130,131,132,133,134,135,256,257,258,259,260,26..., dimensions={0} | all-to-all | bytes 458752 | tf_op jit(solution)/shard_map/all_to_all | solution.py:454
  77.5 0.8 %finish.1 = (f32[512,128]{1,0:T(8,128)}, f32[384,128]{1,0:T(8,128)}) custom-call(bf16[32,28,128]{2,1,0:T(8,128)(2,1)S(1)} %all_to_all.17.got_ref), custom_call_target="tpu_custom_call" | custom-call | tf_op jit(solution)/shard_map/finish/pallas_call | solution.py:455
  (9 shorter events, 0.2 us)
Async XLA Ops:
  2.2 11.9 %collective-permute-start = (bf16[384,640]{1,0:T(8,128)(2,1)S(1)}, bf16[384,640]{1,0:T(8,128)(2,1)S(1)}, u32[]{:S(2)}, u32[]{:S(2)}) collective-permute-start(bf16[384,640]{1,0:T(8,128)(2,1)S(1)} %get-tuple-element.15), channel_id=1, source_target_pairs={{8,16},{24,32},{40,48},{56,64},{72,80},{88,96},{104,112},{120,128}... | collective-permute-start | bytes 1474568 | tf_op jit(solution)/shard_map/ppermute | solution.py:374
  7.6 6.5 %collective-permute-start.1 = (bf16[384,640]{1,0:T(8,128)(2,1)S(1)}, bf16[384,640]{1,0:T(8,128)(2,1)S(1)}, u32[]{:S(2)}, u32[]{:S(2)}) collective-permute-start(bf16[384,640]{1,0:T(8,128)(2,1)S(1)} %get-tuple-element.16), channel_id=1, source_target_pairs={{0,8},{16,24},{32,40},{48,56},{64,72},{80,88},{96,104},{112,120},{... | collective-permute-start | bytes 1474568 | tf_op jit(solution)/shard_map/ppermute | solution.py:375
  11.7 0.7 copy-start
